TPU v7x, 32 devices: a whole 2x2x4 slice. The times are simulated.
32 devices in a mesh: row: 4 (over x, core), col: 8 (over z, y).
Axes of the slice: x: 2, y: 2, z: 4, core: 2. Of those that a mesh axis runs over, the one named last changes fastest.
Arguments:
- pair_density: bfloat16 [2048, 8192], P('col', 'row'), may hold values from -6 to 6
- scale_exp: int32 [2048], replicated, may hold values from -1 to 1
- pair_weight: int32 [2048], replicated, may hold values from 1 to 4
- resident_ids: int32 [512], replicated, may hold values from 0 to 2047, as said below
- diagonal_shift: float32 [8192], replicated, may hold values from 2 to 4
- background: float32 [8192, 8192], P('row', 'col'), as said below
Outputs:
- dielectric: float32 [8192, 8192], P('row', 'col')
- kernel: float32 [2048, 512], P(('col', 'row'))
Inputs may be any that keep to these rules, and one draw needn't show every extreme that they name: `resident_ids`: 512 distinct pair indices. background is symmetric.
All inputs are finite; a program needn't handle non-finite values.
Results may differ from a plain program's by a relative error of at most 0.0003.
Values may be sent and summed in bfloat16 or wider, within the bound.
No kernel may reach another device: no remote copies, remote signals or barrier semaphores. Data moves between devices by JAX's collectives and lax.ppermute only.
A program may use at most 128 MiB of HBM per device.

v0:
```python
import math
import jax
import jax.numpy as jnp
from jax import lax
from jax.sharding import PartitionSpec as P

NG = 8192
SWEEPS = 2
damping = 0.5


def from_root(block, axis, owner):
    block = jnp.where(lax.axis_index(axis) == owner, block, jnp.zeros_like(block))
    return lax.psum(block, axis)


def scale_factor(exponent):
    return jnp.where(exponent < 0, 0.5, jnp.where(exponent > 0, 2.0, 1.0)).astype(jnp.float32)


def pair_contract(left_block, right_block):
    return lax.dot_general(
        left_block, right_block, (((0,), (0,)), ((), ())), preferred_element_type=jnp.float32
    )


def shards(pair_density, scale_exp, pair_weight, resident_ids, diagonal_shift, background):
    row_count = lax.axis_size("row")
    col_count = lax.axis_size("col")
    row_index = lax.axis_index("row")
    col_index = lax.axis_index("col")
    pair_dev, row_width = pair_density.shape
    col_width = background.shape[1]
    pair_total = pair_dev * col_count
    norm_scale = 4 * pair_total
    factor = scale_factor(scale_exp)
    own_factor = lax.dynamic_slice_in_dim(factor, col_index * pair_dev, pair_dev)
    scaled = (pair_density.astype(jnp.float32) * own_factor[:, None]).astype(jnp.bfloat16)
    left_all = lax.all_gather(scaled, "col", axis=0, tiled=True)
    relaid = lax.all_to_all(
        lax.all_to_all(scaled, "row", split_axis=0, concat_axis=1, tiled=True),
        "col",
        split_axis=1,
        concat_axis=0,
        tiled=True,
    )
    share_rows = pair_dev // row_count
    left_order = left_all.reshape(col_count, row_count, share_rows, row_width)
    left_order = left_order.transpose(1, 0, 2, 3).reshape(pair_total, row_width)
    contracted = pair_contract(left_order, lax.all_gather(relaid, "row", axis=0, tiled=True))
    response = contracted / norm_scale
    row_start = row_index * row_width
    col_start = col_index * col_width
    global_rows = row_start + lax.broadcasted_iota(jnp.int32, (row_width, col_width), 0)
    global_cols = col_start + lax.broadcasted_iota(jnp.int32, (row_width, col_width), 1)
    shift_rows = lax.dynamic_slice_in_dim(diagonal_shift, row_start, row_width)
    dielectric = (
        background + response + jnp.where(global_rows == global_cols, shift_rows[:, None], 0.0)
    )
    precond_rows = (
        shift_rows
        + jnp.einsum("pg,pg->g", left_all, left_all, preferred_element_type=jnp.float32)
        / norm_scale
    )
    picked = left_all[resident_ids].astype(jnp.float32) / factor[resident_ids][:, None]
    source_rows = picked.T
    col_ratio = col_count // row_count
    root_row = col_index // col_ratio
    offset = col_index % col_ratio * col_width

    def column_share(values):
        return lax.dynamic_slice_in_dim(values, offset, col_width, 0)

    source_cols, precond_cols = (
        from_root(column_share(source_rows), "row", root_row),
        from_root(column_share(precond_rows), "row", root_row),
    )
    screen_rows = source_rows / precond_rows[:, None]
    screen_cols = source_cols / precond_cols[:, None]
    for sweep_index in range(SWEEPS):
        last_sweep = sweep_index + 1 == SWEEPS
        row_image = lax.psum(
            jnp.dot(dielectric, screen_cols, precision=lax.Precision.HIGHEST), "col"
        )
        if not last_sweep:
            transposed = lax.dot_general(
                dielectric, screen_rows, (((0,), (0,)), ((), ())), precision=lax.Precision.HIGHEST
            )
            col_image = lax.psum(transposed, "row")
            screen_cols = screen_cols + damping * (source_cols - col_image) / precond_cols[:, None]
        screen_rows = screen_rows + damping * (source_rows - row_image) / precond_rows[:, None]
    partial_value = jnp.dot(
        pair_density.astype(jnp.float32), screen_rows, precision=lax.Precision.HIGHEST
    )
    summed = lax.psum_scatter(partial_value, "row", scatter_dimension=0, tiled=True)
    kernel_share = pair_dev // row_count
    weights = lax.dynamic_slice_in_dim(
        pair_weight, col_index * pair_dev + row_index * kernel_share, kernel_share
    ).astype(jnp.float32)
    kernel = weights[:, None] * summed / math.sqrt(NG)
    return (dielectric, kernel)


def solution(mesh):
    return jax.shard_map(
        shards,
        mesh=mesh,
        in_specs=(P("col", "row"), P(), P(), P(), P(), P("row", "col")),
        out_specs=(P("row", "col"), P(("col", "row"), None)),
        check_vma=False,
    )
```

profile of v0, /device:TPU:0, one launch (start us, length us, event | category | flops | bytes accessed | tf_op | source)
XLA Modules:
  0.0 656.9 jit_solution(1160271850657053020)
XLA Ops:
  7.2 0.0 all-gather.3.cloned.1.call-start
  7.2 0.7 select_select_fusion
  7.9 0.1 dynamic_slice.15
  8.0 2.4 multiply_convert_fusion
  10.4 0.0 all-gather.3.cloned.1.call-update
  10.4 0.0 all-gather.5.cloned.1.call-start
  10.5 18.7 %all_to_all.35 = bf16[4,64,2048]{2,1,0:T(8,128)(2,1)S(1)} all-to-all(bf16[4,64,2048]{2,1,0:T(8,128)(2,1)} %bitcast.38), channel_id=1, replica_groups=mesh['row'=4,'col'=8] {'row'}, dimensions={0} | all-to-all | bytes 2097152 | tf_op jit(solution)/shard_map/all_to_all | solution.py:41
  29.2 0.8 copy.14
  30.0 0.0 copy-start.2
  30.0 0.3 all_to_all.29
  30.3 0.6 copy.15
  30.9 51.7 %all_to_all.36 = bf16[64,8,1024]{2,0,1:T(8,128)(2,1)} all-to-all(bf16[64,8,1024]{2,0,1:T(8,128)(2,1)S(1)} %copy.15), channel_id=1, replica_groups=mesh['row'=4,'col'=8] {'col'}, dimensions={1} | all-to-all | bytes 2097152 | tf_op jit(solution)/shard_map/all_to_all | solution.py:40
  82.5 0.0 all-gather.5.cloned.1.call-update
  82.6 0.6 all-reduce.7.cloned.1.call-start
  83.2 0.0 copy-done.2
  83.2 3.1 gather_fusion.1
  86.4 72.6 %all-gather.3.cloned.1.call-done = bf16[2048,2048]{1,0:T(8,128)(2,1)} async-done(((bf16[256,2048]{1,0:T(8,128)(2,1)}), bf16[2048,2048]{1,0:T(8,128)(2,1)}) %all-gather.3.cloned.1.call-update) | async-done | bytes 8388624 | tf_op jit(solution)/shard_map/all_gather | solution.py:39
  159.0 9.7 %gather_fusion = bf16[512,2048]{1,0:T(8,128)(2,1)} fusion(bf16[2048,2048]{1,0:T(8,128)(2,1)} %all-gather.3.cloned.1.call-done, s32[1024]{0:T(1024)S(1)} %pad_clamp_fusion), kind=kCustom, calls=%fused_computation | custom fusion | bytes 4196352 | tf_op jit(solution)/shard_map/gather | solution.py:65
  168.7 2.9 copy.16
  171.6 2.6 convert_element_type.25
  174.1 8.5 %copy.13 = bf16[8,4,64,2048]{3,2,0,1:T(8,128)(2,1)} copy(bf16[8,4,64,2048]{3,2,1,0:T(8,128)(2,1)} %bitcast.37) | data formatting | bytes 16777216 | tf_op jit(solution)/shard_map/reshape | solution.py:48
  182.6 5.2 fusion
  187.8 0.7 multiply_add_fusion
  188.5 4.8 all-gather.5.cloned.1.call-done
  193.2 15.4 %select_add_fusion = f32[2048,1024]{1,0:T(8,128)S(1)} fusion(f32[2048,1024]{1,0:T(8,128)} %param.11, bf16[2048,2048]{1,0:T(8,128)(2,1)} %bitcast.39, bf16[2048,1024]{1,0:T(8,128)(2,1)} %all-gather.5.cloned.1.call-done, f32[2048]{0:T(1024)S(1)} %get-tuple-element.13, s32[1024]{0:T(1024)S(1)} %iota_add_fusion.1, s32[2048]{0:T(1024)S(1)} %iota_add_fusion), kind=kOutput, calls=%fused_computation.4 | convolution fusion | flops 8600420352 | bytes 29380608 | tf_op jit(solution)/shard_map/dot_general | solution.py:22
  208.6 0.0 copy-start.5
  208.6 0.0 copy-start
  208.6 16.1 %fusion.10 = f32[1024,512]{1,0:T(8,128)} fusion(f32[2048,1024]{1,0:T(8,128)S(1)} %select_add_fusion, bf16[512,2048]{0,1:T(8,128)(2,1)S(1)} %copy.16, f32[2048]{0:T(1024)S(1)} %get-tuple-element.12, f32[512]{0:T(512)S(1)} %gather_fusion.1), kind=kOutput, calls=%fused_computation.16 | convolution fusion | flops 12888047616 | bytes 12593152 | tf_op jit(solution)/shard_map/dot_general | solution.py:86
  224.8 0.0 copy-done.5
  224.8 0.0 copy-done
  224.8 1.6 fusion.12
  226.3 0.0 all-reduce.7.cloned.1.call-update
  226.4 0.0 all-reduce.5.cloned.1.call-start
  226.4 5.9 psum.36
  232.3 79.7 %all-reduce.7.cloned.1.call-done = (f32[1024,512]{1,0:T(8,128)}, f32[1024,512]{1,0:T(8,128)}) async-done(((f32[1024,512]{1,0:T(8,128)}, f32[1024,512]{1,0:T(8,128)}), (f32[1024,512]{1,0:T(8,128)}, f32[1024,512]{1,0:T(8,128)})) %all-reduce.7.cloned.1.call-update) | async-done | bytes 4194320 | tf_op jit(solution)/shard_map/psum | solution.py:14
  312.0 0.0 copy-start.3
  312.0 0.0 copy-start.4
  312.0 0.0 copy-start.6
  312.0 18.0 %fusion.30 = f32[2048,512]{1,0:T(8,128)} fusion(f32[2048,1024]{1,0:T(8,128)} %copy-done.5, f32[1024,512]{1,0:T(8,128)} %get-tuple-element.10, f32[1024]{0:T(1024)S(1)} %psum.36), kind=kOutput, calls=%fused_computation.37 | convolution fusion | flops 12885426176 | bytes 14684160 | tf_op jit(solution)/shard_map/dot_general | solution.py:83
  330.0 0.0 copy-done.3
  330.0 0.0 copy-done.4
  330.0 0.0 copy-done.6
  330.0 15.5 %fusion.15 = f32[2048,512]{1,0:T(8,128)} fusion(f32[2048,1024]{1,0:T(8,128)S(1)} %copy-done.6, f32[1024,512]{1,0:T(8,128)S(1)} %copy-done.3, f32[1024,512]{1,0:T(8,128)S(1)} %copy-done.4, f32[1024]{0:T(1024)S(1)} %psum.36), kind=kOutput, calls=%fused_computation.22 | convolution fusion | flops 12887523328 | bytes 16781312 | tf_op jit(solution)/shard_map/dot_general | solution.py:83
  345.5 0.0 copy-start.1
  345.5 0.0 all-reduce.5.cloned.1.call-update
  345.5 0.3 reduce-scatter.4.cloned.1.call-start
  345.8 270.0 %all-reduce.5.cloned.1.call-done = (f32[2048,512]{1,0:T(8,128)}, f32[2048,512]{1,0:T(8,128)}) async-done(((f32[2048,512]{1,0:T(8,128)}, f32[2048,512]{1,0:T(8,128)}), (f32[2048,512]{1,0:T(8,128)}, f32[2048,512]{1,0:T(8,128)})) %all-reduce.5.cloned.1.call-update) | async-done | bytes 8388624 | tf_op jit(solution)/shard_map/psum | solution.py:82
  615.9 0.0 copy-done.1
  615.9 9.4 %fusion.25 = f32[256,512]{0,1:T(8,128)} fusion(bf16[256,2048]{1,0:T(8,128)(2,1)S(1)} %copy-done.1, f32[2048,512]{1,0:T(8,128)} %get-tuple-element.8, f32[2048,512]{1,0:T(8,128)} %get-tuple-element.9, bf16[512,2048]{0,1:T(8,128)(2,1)S(1)} %copy.16, f32[2048]{0:T(1024)S(1)} %get-tuple-element.12, f32[512]{0:T(512)S(1)} %gather_fusion.1), kind=kOutput, calls=%fused_computation.33 | convolution fusion | flops 3233808384 | bytes 12068864 | tf_op jit(solution)/shard_map/dot_general | solution.py:92
  625.3 2.0 copy.24
  627.3 0.0 reduce-scatter.4.cloned.1.call-update
  627.4 0.8 dynamic-slice_convert_fusion
  628.1 20.1 %reduce-scatter.4.cloned.1.call-done = f32[64,512]{1,0:T(8,128)} async-done(((f32[256,512]{1,0:T(8,128)}), f32[64,512]{1,0:T(8,128)}) %reduce-scatter.4.cloned.1.call-update) | async-done | bytes 131088
  648.3 1.0 copy.25
  649.3 0.8 copy.17
  (6 shorter events, 0.1 us)
Async XLA Ops:
  7.2 151.8 %all-gather.3.cloned.1.call-start = ((), (), s32[]{:S(2)}) async-start(), calls=%async_computation.3 | async-start | bytes 9437184 | tf_op jit(solution)/shard_map/all_gather | solution.py:39
  10.4 182.8 %all-gather.5.cloned.1.call-start = ((), (), s32[]{:S(2)}) async-start(), calls=%async_computation.4 | async-start | bytes 5242880 | tf_op jit(solution)/shard_map/all_gather | solution.py:50
  30.0 53.2 %copy-start.2 = (s32[512]{0:T(512)S(1)}, s32[512]{0:T(512)}, u32[]{:S(2)}) copy-start(s32[512]{0:T(512)} %param.9) | copy-start | bytes 6148
  82.6 229.5 %all-reduce.7.cloned.1.call-start = ((), (), s32[]{:S(2)}) async-start(), calls=%async_computation.7 | async-start | bytes 8388608 | tf_op jit(solution)/shard_map/psum | solution.py:14
  208.6 16.1 %copy-start.5 = (f32[2048,1024]{1,0:T(8,128)}, f32[2048,1024]{1,0:T(8,128)S(1)}, u32[]{:S(2)}) copy-start(f32[2048,1024]{1,0:T(8,128)S(1)} %select_add_fusion) | copy-start | bytes 25165828
  208.6 16.1 %copy-start = (f32[512,2048]{0,1:T(8,128)S(1)}, f32[512,2048]{0,1:T(8,128)}, u32[]{:S(2)}) copy-start(f32[512,2048]{0,1:T(8,128)} %convert_element_type.25) | copy-start | bytes 12582916
  226.4 389.5 %all-reduce.5.cloned.1.call-start = ((), (), s32[]{:S(2)}) async-start(), calls=%async_computation.6 | async-start | bytes 16777216 | tf_op jit(solution)/shard_map/psum | solution.py:82
  312.0 18.0 %copy-start.3 = (f32[1024,512]{1,0:T(8,128)S(1)}, f32[1024,512]{1,0:T(8,128)}, u32[]{:S(2)}) copy-start(f32[1024,512]{1,0:T(8,128)} %get-tuple-element.10) | copy-start | bytes 6291460
  312.0 18.0 %copy-start.4 = (f32[1024,512]{1,0:T(8,128)S(1)}, f32[1024,512]{1,0:T(8,128)}, u32[]{:S(2)}) copy-start(f32[1024,512]{1,0:T(8,128)} %get-tuple-element.11) | copy-start | bytes 6291460
  312.0 18.0 %copy-start.6 = (f32[2048,1024]{1,0:T(8,128)S(1)}, f32[2048,1024]{1,0:T(8,128)}, u32[]{:S(2)}) copy-start(f32[2048,1024]{1,0:T(8,128)} %copy-done.5) | copy-start | bytes 25165828
  345.5 270.4 %copy-start.1 = (bf16[256,2048]{1,0:T(8,128)(2,1)S(1)}, bf16[256,2048]{1,0:T(8,128)(2,1)}, u32[]{:S(2)}) copy-start(bf16[256,2048]{1,0:T(8,128)(2,1)} %param.6) | copy-start | bytes 3145732
  345.5 302.7 %reduce-scatter.4.cloned.1.call-start = ((), (), s32[]{:S(2)}) async-start(), calls=%async_computation.5 | async-start | bytes 655360
Sparse Core Ops, SparseCore 0:
  10.7 148.2 all-gather.2
  160.6 32.6 all-gather.4
  226.5 85.5 all-reduce.6
  345.6 270.1 all-reduce.4
  627.5 20.7 reduce-scatter.3
where the time goes:
time: 660 us; the launch traced here: 657 us
  waiting for transfers between devices  447 us (68%)
  blocking collectives  76.2 us (12%)
  matrix products  74.4 us (11%)
  local copies, waits for them, and re-layouts  29.8 us (5%)
  between operations  14.2 us (2%)
  other arithmetic  13.9 us (2%)
    psum x1, waiting for transfers between devices, shards(): lax.psum(jnp.dot(dielectric, screen_cols, precision=lax.Precision.HIGHEST...  270 us
    psum x1, waiting for transfers between devices, from_root(): return lax.psum(block, axis)  79.7 us
    all_gather x1, waiting for transfers between devices, shards(): left_all = lax.all_gather(scaled, 'col', axis=0, tiled=True)  72.6 us
    all_to_all x1, blocking collectives, shards(): lax.all_to_all(lax.all_to_all(scaled, 'row', split_axis=0, concat_axis=1,...  51.7 us
    dot_general x2, matrix products, shards(): jnp.dot(dielectric, screen_cols, precision=lax.Precision.HIGHEST)  33.4 us
    unnamed x6, waiting for transfers between devices  20.2 us
    all_to_all x1, blocking collectives, shards(): lax.all_to_all(scaled, 'row', split_axis=0, concat_axis=1, tiled=True)  18.7 us
    dot_general x1, matrix products, shards(): lax.dot_general(dielectric, screen_rows, (((0,), (0,)), ((), ())), precis...  16.1 us
  transfers between devices with their start and end apart: 5, of which 5 were waited for; matrix products, arithmetic and copies ran while one was open for 5% of the time, Pallas kernels for 0%

commit v1 on v0

--- a/solution.py
+++ b/solution.py
@@ -36,7 +36,12 @@
     factor = scale_factor(scale_exp)
     own_factor = lax.dynamic_slice_in_dim(factor, col_index * pair_dev, pair_dev)
     scaled = (pair_density.astype(jnp.float32) * own_factor[:, None]).astype(jnp.bfloat16)
-    left_all = lax.all_gather(scaled, "col", axis=0, tiled=True)
+    ring = [scaled]
+    for hop in range(7):
+        ring.append(lax.ppermute(ring[-1], "col", [(dev, (dev + 1) % 8) for dev in range(8)]))
+    left_all = jnp.roll(
+        jnp.concatenate(ring[::-1], axis=0), (lax.axis_index("col") + 1) * ring[0].shape[0], axis=0
+    )
     relaid = lax.all_to_all(
         lax.all_to_all(scaled, "row", split_axis=0, concat_axis=1, tiled=True),
         "col",

time: 660 us -> 744 us (1.13)
  waiting for transfers between devices: 447 us -> 543 us
  blocking collectives: 76.2 us -> 5.67 us
  local copies, waits for them, and re-layouts: 29.8 us -> 67.2 us
  starting transfers between devices: 0.98 us -> 16.7 us
    ppermute x0 -> x7, waiting for transfers between devices: none -> 169 us  [shards(): lax.ppermute(ring[-1], 'col', [(dev, (dev + 1) % 8) for dev in range(8)])]
    all_gather x1 -> x0, waiting for transfers between devices: 72.6 us -> none  [shards(): left_all = lax.all_gather(scaled, 'col', axis=0, tiled=True)]
    all_to_all x2 -> x0, blocking collectives: 70.3 us -> none  [the longest x1 51.7 us: shards(): lax.all_to_all(lax.all_to_all(scaled, 'row', split_axis=0, concat_axis=1,...]
    unnamed x17 -> x31, local copies, waits for them, and re-layouts: 3.87 us -> 35.1 us
    all_to_all x0 -> x2, starting transfers between devices: none -> 10.2 us  [the longest x1 6 us: shards(): lax.all_to_all(lax.all_to_all(scaled, 'row', split_axis=0, concat_axis=1,...]
    reshape x1 -> x0, local copies, waits for them, and re-layouts: 8.48 us -> none  [shards(): left_order = left_all.reshape(col_count, row_count, share_rows, row_width)]
    transpose x0 -> x1, local copies, waits for them, and re-layouts: none -> 8.29 us  [shards(): left_order = left_order.transpose(1, 0, 2, 3).reshape(pair_total, row_width)]
    unnamed x6 -> x5, waiting for transfers between devices: 20.2 us -> 20.2 us
  transfers between devices with their start and end apart: 5 -> 13, of which waited for: 5 -> 10; matrix products, arithmetic and copies ran while one was open for 5% -> 10% of each run, Pallas kernels for 0% -> 0%
where the time goes in v1:
time: 744 us; the launch traced here: 740 us
  waiting for transfers between devices  543 us (73%)
  matrix products  74.4 us (10%)
  local copies, waits for them, and re-layouts  67.2 us (9%)
  other arithmetic  18.6 us (3%)
  starting transfers between devices  16.7 us (2%)
  between operations  14.4 us (2%)
    psum x1, waiting for transfers between devices, shards(): lax.psum(jnp.dot(dielectric, screen_cols, precision=lax.Precision.HIGHEST...  270 us
    ppermute x7, waiting for transfers between devices, shards(): lax.ppermute(ring[-1], 'col', [(dev, (dev + 1) % 8) for dev in range(8)])  169 us
    psum x1, waiting for transfers between devices, from_root(): return lax.psum(block, axis)  84.5 us
    unnamed x31, local copies, waits for them, and re-layouts  35.1 us
    dot_general x2, matrix products, shards(): jnp.dot(dielectric, screen_cols, precision=lax.Precision.HIGHEST)  33.5 us
    unnamed x5, waiting for transfers between devices  20.2 us
    dot_general x1, matrix products, shards(): lax.dot_general(dielectric, screen_rows, (((0,), (0,)), ((), ())), precis...  16.1 us
    dot_general x1, matrix products, pair_contract(): lax.dot_general(left_block, right_block, (((0,), (0,)), ((), ())), prefer...  15.4 us
  transfers between devices with their start and end apart: 13, of which 10 were waited for; matrix products, arithmetic and copies ran while one was open for 10% of the time, Pallas kernels for 0%

profile of v1, /device:TPU:0, one launch (start us, length us, event | category | flops | bytes accessed | tf_op | source)
XLA Modules:
  0.0 740.3 jit_solution(437090732018930095)
XLA Ops:
  7.2 0.7 select_select_fusion
  7.9 0.1 dynamic_slice.19
  7.9 1.5 multiply_convert_fusion
  9.4 0.0 copy-start.1
  9.4 3.0 collective-permute-start
  12.5 26.2 %collective-permute-done = bf16[256,2048]{1,0:T(8,128)(2,1)S(1)} collective-permute-done((bf16[256,2048]{1,0:T(8,128)(2,1)S(1)}, bf16[256,2048]{1,0:T(8,128)(2,1)S(1)}, u32[]{:S(2)}, u32[]{:S(2)}) %collective-permute-start) | collective-permute-done | bytes 1048608 | tf_op jit(solution)/shard_map/ppermute | solution.py:41
  38.7 27.0 %collective-permute-done.1 = bf16[256,2048]{1,0:T(8,128)(2,1)S(1)} collective-permute-done((bf16[256,2048]{1,0:T(8,128)(2,1)S(1)}, bf16[256,2048]{1,0:T(8,128)(2,1)S(1)}, u32[]{:S(2)}, u32[]{:S(2)}) %collective-permute-start.1) | collective-permute-done | bytes 1048608 | tf_op jit(solution)/shard_map/ppermute | solution.py:41
  65.7 26.3 %collective-permute-done.2 = bf16[256,2048]{1,0:T(8,128)(2,1)} collective-permute-done((bf16[256,2048]{1,0:T(8,128)(2,1)S(1)}, bf16[256,2048]{1,0:T(8,128)(2,1)}, u32[]{:S(2)}, u32[]{:S(2)}) %collective-permute-start.2) | collective-permute-done | bytes 1048608 | tf_op jit(solution)/shard_map/ppermute | solution.py:41
  92.0 4.2 all-to-all-start
  96.2 21.4 %collective-permute-done.3 = bf16[256,2048]{1,0:T(8,128)(2,1)} collective-permute-done((bf16[256,2048]{1,0:T(8,128)(2,1)}, bf16[256,2048]{1,0:T(8,128)(2,1)}, u32[]{:S(2)}, u32[]{:S(2)}) %collective-permute-start.3) | collective-permute-done | bytes 1048608 | tf_op jit(solution)/shard_map/ppermute | solution.py:41
  117.6 3.0 copy.18
  120.6 2.2 all_to_all.29
  122.8 2.8 copy.19
  125.5 6.0 all-to-all-start.1
  131.5 0.0 all-gather.2.cloned.1.call-start
  131.6 16.9 %collective-permute-done.4 = bf16[256,2048]{1,0:T(8,128)(2,1)} collective-permute-done((bf16[256,2048]{1,0:T(8,128)(2,1)}, bf16[256,2048]{1,0:T(8,128)(2,1)}, u32[]{:S(2)}, u32[]{:S(2)}) %collective-permute-start.4) | collective-permute-done | bytes 1048608 | tf_op jit(solution)/shard_map/ppermute | solution.py:41
  148.5 2.5 collective-permute-start.5
  151.0 30.8 %collective-permute-done.5 = bf16[256,2048]{1,0:T(8,128)(2,1)} collective-permute-done((bf16[256,2048]{1,0:T(8,128)(2,1)}, bf16[256,2048]{1,0:T(8,128)(2,1)}, u32[]{:S(2)}, u32[]{:S(2)}) %collective-permute-start.5) | collective-permute-done | bytes 1048608 | tf_op jit(solution)/shard_map/ppermute | solution.py:41
  181.8 0.0 all-gather.2.cloned.1.call-update
  181.8 0.6 all-reduce.7.cloned.1.call-start
  182.4 3.1 gather_fusion.1
  185.7 20.1 %collective-permute-done.6 = bf16[256,2048]{1,0:T(8,128)(2,1)} collective-permute-done((bf16[256,2048]{1,0:T(8,128)(2,1)}, bf16[256,2048]{1,0:T(8,128)(2,1)}, u32[]{:S(2)}, u32[]{:S(2)}) %collective-permute-start.6) | collective-permute-done | bytes 1048608 | tf_op jit(solution)/shard_map/ppermute | solution.py:41
  205.8 2.3 constant_dynamic-update-slice_fusion.15
  208.1 2.3 constant_dynamic-update-slice_fusion.14
  210.4 2.3 constant_dynamic-update-slice_fusion.13
  212.7 2.5 constant_dynamic-update-slice_fusion.12
  215.2 2.5 constant_dynamic-update-slice_fusion.11
  217.7 1.1 constant_dynamic-update-slice_fusion.10
  218.8 1.0 constant_dynamic-update-slice_fusion.9
  219.8 1.3 constant_dynamic-update-slice_fusion.8
  221.1 2.4 constant_dynamic-update-slice_fusion.7
  223.5 2.4 constant_dynamic-update-slice_fusion.6
  225.9 2.3 constant_dynamic-update-slice_fusion.5
  228.2 2.3 constant_dynamic-update-slice_fusion.4
  230.5 2.4 constant_dynamic-update-slice_fusion.3
  232.9 1.1 constant_dynamic-update-slice_fusion.2
  233.9 1.1 constant_dynamic-update-slice_fusion.1
  235.0 1.2 constant_dynamic-update-slice_fusion
  236.2 10.2 %fusion = (f32[2048]{0:T(1024)S(1)}, bf16[2048,2048]{1,0:T(8,128)(2,1)}) fusion(bf16[4096,2048]{1,0:T(8,128)(2,1)} %constant_dynamic-update-slice_fusion, s32[]{:T(128)S(6)} %select_n.75), kind=kLoop, calls=%fused_computation.3 | loop fusion | flops 12580864 | bytes 16785412 | tf_op jit(solution)/shard_map/pg,pg->g/dot_general | solution.py:67
  246.4 9.7 %gather_fusion = bf16[512,2048]{1,0:T(8,128)(2,1)} fusion(bf16[2048,2048]{1,0:T(8,128)(2,1)} %get-tuple-element.17, s32[1024]{0:T(1024)S(1)} %pad_clamp_fusion), kind=kCustom, calls=%fused_computation | custom fusion | bytes 4196352 | tf_op jit(solution)/shard_map/gather | solution.py:70
  256.1 8.3 %copy.17 = bf16[4,8,64,2048]{3,2,1,0:T(8,128)(2,1)} copy(bf16[4,8,64,2048]{3,2,0,1:T(8,128)(2,1)} %bitcast.37) | data formatting | bytes 16777216 | tf_op jit(solution)/shard_map/transpose | solution.py:54
  264.4 2.9 copy.20
  267.2 0.6 convert_element_type.25
  267.8 0.7 multiply_add_fusion
  268.5 1.7 fusion.12
  270.2 15.4 %select_add_fusion = f32[2048,1024]{1,0:T(8,128)S(1)} fusion(f32[2048,1024]{1,0:T(8,128)} %param.11, bf16[2048,2048]{1,0:T(8,128)(2,1)} %bitcast.38, bf16[2048,1024]{1,0:T(8,128)(2,1)} %all-gather.2.cloned.1.call-done, f32[2048]{0:T(1024)S(1)} %get-tuple-element.15, s32[1024]{0:T(1024)S(1)} %iota_add_fusion.1, s32[2048]{0:T(1024)S(1)} %iota_add_fusion), kind=kOutput, calls=%fused_computation.4 | convolution fusion | flops 8600420352 | bytes 29380608 | tf_op jit(solution)/shard_map/dot_general | solution.py:22
  285.6 3.4 copy-done.5
  289.0 16.1 %fusion.10 = f32[1024,512]{1,0:T(8,128)} fusion(f32[2048,1024]{1,0:T(8,128)S(1)} %select_add_fusion, bf16[512,2048]{0,1:T(8,128)(2,1)S(1)} %copy.20, f32[2048]{0:T(1024)S(1)} %get-tuple-element.14, f32[512]{0:T(512)S(1)} %gather_fusion.1), kind=kOutput, calls=%fused_computation.16 | convolution fusion | flops 12888047616 | bytes 12593152 | tf_op jit(solution)/shard_map/dot_general | solution.py:91
  305.1 0.0 all-reduce.7.cloned.1.call-update
  305.1 0.0 all-reduce.5.cloned.1.call-start
  305.2 5.7 psum.36
  310.8 84.5 %all-reduce.7.cloned.1.call-done = (f32[1024,512]{1,0:T(8,128)}, f32[1024,512]{1,0:T(8,128)}) async-done(((f32[1024,512]{1,0:T(8,128)}, f32[1024,512]{1,0:T(8,128)}), (f32[1024,512]{1,0:T(8,128)}, f32[1024,512]{1,0:T(8,128)})) %all-reduce.7.cloned.1.call-update) | async-done | bytes 4194320 | tf_op jit(solution)/shard_map/psum | solution.py:14
  395.3 18.0 %fusion.30 = f32[2048,512]{1,0:T(8,128)} fusion(f32[2048,1024]{1,0:T(8,128)} %copy-done.5, f32[1024,512]{1,0:T(8,128)} %get-tuple-element.12, f32[1024]{0:T(1024)S(1)} %psum.36), kind=kOutput, calls=%fused_computation.37 | convolution fusion | flops 12885426176 | bytes 14684160 | tf_op jit(solution)/shard_map/dot_general | solution.py:88
  413.3 15.5 %fusion.15 = f32[2048,512]{1,0:T(8,128)} fusion(f32[2048,1024]{1,0:T(8,128)S(1)} %copy-done.6, f32[1024,512]{1,0:T(8,128)S(1)} %copy-done.3, f32[1024,512]{1,0:T(8,128)S(1)} %copy-done.4, f32[1024]{0:T(1024)S(1)} %psum.36), kind=kOutput, calls=%fused_computation.22 | convolution fusion | flops 12887523328 | bytes 16781312 | tf_op jit(solution)/shard_map/dot_general | solution.py:88
  428.8 0.0 all-reduce.5.cloned.1.call-update
  428.8 0.3 reduce-scatter.4.cloned.1.call-start
  429.1 270.0 %all-reduce.5.cloned.1.call-done = (f32[2048,512]{1,0:T(8,128)}, f32[2048,512]{1,0:T(8,128)}) async-done(((f32[2048,512]{1,0:T(8,128)}, f32[2048,512]{1,0:T(8,128)}), (f32[2048,512]{1,0:T(8,128)}, f32[2048,512]{1,0:T(8,128)})) %all-reduce.5.cloned.1.call-update) | async-done | bytes 8388624 | tf_op jit(solution)/shard_map/psum | solution.py:87
  699.1 9.4 %fusion.25 = f32[256,512]{0,1:T(8,128)} fusion(bf16[256,2048]{1,0:T(8,128)(2,1)S(1)} %copy-done, f32[2048,512]{1,0:T(8,128)} %get-tuple-element.10, f32[2048,512]{1,0:T(8,128)} %get-tuple-element.11, bf16[512,2048]{0,1:T(8,128)(2,1)S(1)} %copy.20, f32[2048]{0:T(1024)S(1)} %get-tuple-element.14, f32[512]{0:T(512)S(1)} %gather_fusion.1), kind=kOutput, calls=%fused_computation.33 | convolution fusion | flops 3233808384 | bytes 12068864 | tf_op jit(solution)/shard_map/dot_general | solution.py:97
  708.5 2.0 copy.28
  710.6 0.0 reduce-scatter.4.cloned.1.call-update
  710.6 0.8 dynamic-slice_convert_fusion
  711.4 20.1 %reduce-scatter.4.cloned.1.call-done = f32[64,512]{1,0:T(8,128)} async-done(((f32[256,512]{1,0:T(8,128)}), f32[64,512]{1,0:T(8,128)}) %reduce-scatter.4.cloned.1.call-update) | async-done | bytes 131088
  731.5 1.0 copy.29
  732.6 0.8 copy.21
  (26 shorter events, 0.1 us)
Async XLA Ops:
  9.4 82.6 %copy-start.1 = (bf16[256,2048]{1,0:T(8,128)(2,1)}, bf16[256,2048]{1,0:T(8,128)(2,1)S(1)}, u32[]{:S(2)}) copy-start(bf16[256,2048]{1,0:T(8,128)(2,1)S(1)} %multiply_convert_fusion) | copy-start | bytes 3145732
  9.4 29.2 %collective-permute-start = (bf16[256,2048]{1,0:T(8,128)(2,1)S(1)}, bf16[256,2048]{1,0:T(8,128)(2,1)S(1)}, u32[]{:S(2)}, u32[]{:S(2)}) collective-permute-start(bf16[256,2048]{1,0:T(8,128)(2,1)S(1)} %multiply_convert_fusion), channel_id=1, source_target_pairs={{0,1},{1,2},{2,3},{3,4},{4,5},{5,6},{6,7},{7,0},{8,9},{9,10},{10,1... | collective-permute-start | bytes 3145736 | tf_op jit(solution)/shard_map/ppermute | solution.py:41
  38.7 27.0 %collective-permute-start.1 = (bf16[256,2048]{1,0:T(8,128)(2,1)S(1)}, bf16[256,2048]{1,0:T(8,128)(2,1)S(1)}, u32[]{:S(2)}, u32[]{:S(2)}) collective-permute-start(bf16[256,2048]{1,0:T(8,128)(2,1)S(1)} %collective-permute-done), channel_id=1, source_target_pairs={{0,1},{1,2},{2,3},{3,4},{4,5},{5,6},{6,7},{7,0},{8,9},{9,10},{10,1... | collective-permute-start | bytes 3145736 | tf_op jit(solution)/shard_map/ppermute | solution.py:41
  65.7 26.3 %collective-permute-start.2 = (bf16[256,2048]{1,0:T(8,128)(2,1)S(1)}, bf16[256,2048]{1,0:T(8,128)(2,1)}, u32[]{:S(2)}, u32[]{:S(2)}) collective-permute-start(bf16[256,2048]{1,0:T(8,128)(2,1)S(1)} %collective-permute-done.1), channel_id=1, source_target_pairs={{0,1},{1,2},{2,3},{3,4},{4,5},{5,6},{6,7},{7,0},{8,9},{9,10},{10,1... | collective-permute-start | bytes 3145736 | tf_op jit(solution)/shard_map/ppermute | solution.py:41
  92.0 25.6 %collective-permute-start.3 = (bf16[256,2048]{1,0:T(8,128)(2,1)}, bf16[256,2048]{1,0:T(8,128)(2,1)}, u32[]{:S(2)}, u32[]{:S(2)}) collective-permute-start(bf16[256,2048]{1,0:T(8,128)(2,1)} %collective-permute-done.2), channel_id=1, source_target_pairs={{0,1},{1,2},{2,3},{3,4},{4,5},{5,6},{6,7},{7,0},{8,9},{9,10},{10,1... | collective-permute-start | bytes 3145736 | tf_op jit(solution)/shard_map/ppermute | solution.py:41
  92.0 25.6 %all-to-all-start = ((bf16[4,64,2048]{2,1,0:T(8,128)(2,1)}), bf16[4,64,2048]{2,1,0:T(8,128)(2,1)}, u32[]{:S(2)}, u32[]{:S(2)}) async-start(bf16[4,64,2048]{2,1,0:T(8,128)(2,1)} %bitcast.39), calls=%async_computation | async-start | bytes 2097152 | tf_op jit(solution)/shard_map/all_to_all | solution.py:46
  117.6 30.9 %collective-permute-start.4 = (bf16[256,2048]{1,0:T(8,128)(2,1)}, bf16[256,2048]{1,0:T(8,128)(2,1)}, u32[]{:S(2)}, u32[]{:S(2)}) collective-permute-start(bf16[256,2048]{1,0:T(8,128)(2,1)} %collective-permute-done.3), channel_id=1, source_target_pairs={{0,1},{1,2},{2,3},{3,4},{4,5},{5,6},{6,7},{7,0},{8,9},{9,10},{10,1... | collective-permute-start | bytes 3145736 | tf_op jit(solution)/shard_map/ppermute | solution.py:41
  120.6 61.8 %copy-start.2 = (s32[512]{0:T(512)S(1)}, s32[512]{0:T(512)}, u32[]{:S(2)}) copy-start(s32[512]{0:T(512)} %param.9) | copy-start | bytes 6148
  125.5 56.2 %all-to-all-start.1 = ((bf16[64,8,1024]{2,0,1:T(8,128)(2,1)}), bf16[64,8,1024]{2,0,1:T(8,128)(2,1)}, u32[]{:S(2)}, u32[]{:S(2)}) async-start(bf16[64,8,1024]{2,0,1:T(8,128)(2,1)} %copy.19), calls=%async_computation.1 | async-start | bytes 2097152 | tf_op jit(solution)/shard_map/all_to_all | solution.py:45
  131.5 138.6 %all-gather.2.cloned.1.call-start = ((), (), s32[]{:S(2)}) async-start(), calls=%async_computation.3 | async-start | bytes 5242880 | tf_op jit(solution)/shard_map/all_gather | solution.py:55
  148.5 33.3 %collective-permute-start.5 = (bf16[256,2048]{1,0:T(8,128)(2,1)}, bf16[256,2048]{1,0:T(8,128)(2,1)}, u32[]{:S(2)}, u32[]{:S(2)}) collective-permute-start(bf16[256,2048]{1,0:T(8,128)(2,1)} %collective-permute-done.4), channel_id=1, source_target_pairs={{0,1},{1,2},{2,3},{3,4},{4,5},{5,6},{6,7},{7,0},{8,9},{9,10},{10,1... | collective-permute-start | bytes 3145736 | tf_op jit(solution)/shard_map/ppermute | solution.py:41
  181.8 24.0 %collective-permute-start.6 = (bf16[256,2048]{1,0:T(8,128)(2,1)}, bf16[256,2048]{1,0:T(8,128)(2,1)}, u32[]{:S(2)}, u32[]{:S(2)}) collective-permute-start(bf16[256,2048]{1,0:T(8,128)(2,1)} %collective-permute-done.5), channel_id=1, source_target_pairs={{0,1},{1,2},{2,3},{3,4},{4,5},{5,6},{6,7},{7,0},{8,9},{9,10},{10,1... | collective-permute-start | bytes 3145736 | tf_op jit(solution)/shard_map/ppermute | solution.py:41
  181.8 213.5 %all-reduce.7.cloned.1.call-start = ((), (), s32[]{:S(2)}) async-start(), calls=%async_computation.6 | async-start | bytes 8388608 | tf_op jit(solution)/shard_map/psum | solution.py:14
  212.7 7.1 copy-start
  285.6 3.4 copy-start.5
  305.1 394.0 %all-reduce.5.cloned.1.call-start = ((), (), s32[]{:S(2)}) async-start(), calls=%async_computation.5 | async-start | bytes 16777216 | tf_op jit(solution)/shard_map/psum | solution.py:87
  395.3 18.0 %copy-start.3 = (f32[1024,512]{1,0:T(8,128)S(1)}, f32[1024,512]{1,0:T(8,128)}, u32[]{:S(2)}) copy-start(f32[1024,512]{1,0:T(8,128)} %get-tuple-element.12) | copy-start | bytes 6291460
  395.3 18.0 %copy-start.4 = (f32[1024,512]{1,0:T(8,128)S(1)}, f32[1024,512]{1,0:T(8,128)}, u32[]{:S(2)}) copy-start(f32[1024,512]{1,0:T(8,128)} %get-tuple-element.13) | copy-start | bytes 6291460
  395.3 18.0 %copy-start.6 = (f32[2048,1024]{1,0:T(8,128)S(1)}, f32[2048,1024]{1,0:T(8,128)}, u32[]{:S(2)}) copy-start(f32[2048,1024]{1,0:T(8,128)} %copy-done.5) | copy-start | bytes 25165828
  428.8 302.7 %reduce-scatter.4.cloned.1.call-start = ((), (), s32[]{:S(2)}) async-start(), calls=%async_computation.4 | async-start | bytes 655360
Sparse Core Ops, SparseCore 0:
  181.9 59.2 all-gather.1
  305.2 90.0 all-reduce.6
  428.9 270.1 all-reduce.4
  710.7 20.7 reduce-scatter.3
